TPU v7x, 512 devices: a whole 4x8x8 slice. The times are simulated.
512 devices in a mesh: tgt: 16 (over z, x_lo), sup: 32 (over y, x_hi, core).
Axes of the slice: x: 4 (x_hi: 2, x_lo: 2; x = x_hi * 2 + x_lo), y: 8, z: 8, core: 2. Of those that a mesh axis runs over, the one named last changes fastest.
Arguments:
- cross_kernel: bfloat16 [32, 32, 512, 512], P('tgt', 'sup'), may hold values from -6 to 6
- cotangent: bfloat16 [32, 32, 512, 512], P('tgt', 'sup'), may hold values from -6 to 6
- self_tgt: bfloat16 [32, 512, 512], P('tgt', 'sup'), may hold values from -320 to 320
- self_sup: bfloat16 [32, 512, 512], P('sup', 'tgt'), may hold values from -320 to 320
Outputs:
- kernel_out: bfloat16 [32, 32, 512, 512], P('tgt', 'sup')
- grad_cross: bfloat16 [32, 32, 512, 512], P('tgt', 'sup')
- grad_self_tgt: float32 [32, 512, 512], P('tgt', 'sup')
- grad_self_sup: float32 [32, 512, 512], P('sup', 'tgt')
All inputs are finite; a program needn't handle non-finite values.
Results may differ from a plain program's by a relative error of at most 0.02.
Values may be sent and summed in bfloat16 or wider, within the bound.
A program may use at most 64 MiB of HBM per device.

v0:
```python
import jax
import jax.numpy as jnp
from jax import lax
from jax.sharding import PartitionSpec as P


def softmax_rows(scores):
    return jax.nn.softmax(scores.astype(jnp.float32), axis=-1).astype(jnp.bfloat16)


def soft_back(probs, dprobs):
    weights = probs.astype(jnp.float32)
    return weights * (dprobs - jnp.sum(dprobs * weights, axis=-1, keepdims=True))


def body(cross_kernel, cotangent, self_tgt, self_sup):
    rows_tgt = self_tgt.shape[1]
    rows_sup = self_sup.shape[1]
    probs_tgt = lax.all_gather(softmax_rows(self_tgt), "sup", axis=1, tiled=True)
    probs_sup = lax.all_gather(softmax_rows(self_sup), "tgt", axis=1, tiled=True)
    mixture = jnp.einsum(
        "tskl,sjl->tskj", cross_kernel, probs_sup, preferred_element_type=jnp.float32
    ).astype(jnp.bfloat16)
    kernel_out = jnp.einsum(
        "tik,tskj->tsij", probs_tgt, mixture, preferred_element_type=jnp.float32
    ).astype(jnp.bfloat16)
    left_side = jnp.einsum(
        "tik,tskl->tsil", probs_tgt, cross_kernel, preferred_element_type=jnp.float32
    ).astype(jnp.bfloat16)
    held_grad = jnp.einsum(
        "tsik,skl->tsil", cotangent, probs_sup, preferred_element_type=jnp.float32
    ).astype(jnp.bfloat16)
    grad_cross = jnp.einsum(
        "tki,tskl->tsil", probs_tgt, held_grad, preferred_element_type=jnp.float32
    ).astype(jnp.bfloat16)
    dprob_tgt = jnp.einsum("tsik,tsjk->tij", cotangent, mixture, preferred_element_type=jnp.float32)
    dprob_sup = jnp.einsum(
        "tsij,tsil->sjl", cotangent, left_side, preferred_element_type=jnp.float32
    )
    summed_tgt = lax.psum_scatter(dprob_tgt, "sup", scatter_dimension=1, tiled=True)
    summed_sup = lax.psum_scatter(dprob_sup, "tgt", scatter_dimension=1, tiled=True)
    owned_tgt = lax.dynamic_slice_in_dim(probs_tgt, lax.axis_index("sup") * rows_tgt, rows_tgt, 1)
    owned_sup = lax.dynamic_slice_in_dim(probs_sup, lax.axis_index("tgt") * rows_sup, rows_sup, 1)
    grad_self_tgt = soft_back(owned_tgt, summed_tgt)
    grad_self_sup = soft_back(owned_sup, summed_sup)
    return (kernel_out, grad_cross, grad_self_tgt, grad_self_sup)


def solution(mesh):
    in_specs = (
        P("tgt", "sup", None, None),
        P("tgt", "sup", None, None),
        P("tgt", "sup", None),
        P("sup", "tgt", None),
    )
    out_specs = (
        P("tgt", "sup", None, None),
        P("tgt", "sup", None, None),
        P("tgt", "sup", None),
        P("sup", "tgt", None),
    )
    return jax.shard_map(body, mesh=mesh, in_specs=in_specs, out_specs=out_specs, check_vma=False)
```

profile of v0, /device:TPU:8, one launch (start us, length us, event | category | flops | bytes accessed | tf_op | source)
XLA Modules:
  0.0 315.7 jit_solution(5673152142917007174)
XLA Ops:
  7.2 0.0 copy-start
  7.2 0.0 all-gather.2.cloned.1.call-start
  7.2 0.9 reduce_max.30
  8.2 0.9 fusion.20
  9.1 1.5 divide_convert_fusion
  10.6 0.0 all-gather.2.cloned.1.call-update
  10.6 0.0 reduce-scatter.3.cloned.1.call-start
  10.6 0.9 reduce_max.28
  11.5 1.0 fusion.21
  12.5 0.9 divide_convert_fusion.1
  13.3 42.3 %all_gather.6 = bf16[1,512,512]{2,1,0:T(8,128)(2,1)S(1)} all-gather(bf16[1,32,512]{2,1,0:T(8,128)(2,1)S(1)} %divide_convert_fusion.1), channel_id=1, replica_groups=mesh['tgt'=16,'sup'=32] {'tgt'}, dimensions={1}, use_global_device_ids=true | all-gather | bytes 557056 | tf_op jit(solution)/shard_map/all_gather | solution.py:20
  55.6 0.8 copy-done.2
  56.4 2.0 fusion.3
  58.4 0.0 copy-done
  58.4 2.1 convolution_bitcast_fusion
  60.4 0.0 reduce-scatter.3.cloned.1.call-update
  60.5 0.0 reduce-scatter.5.cloned.1.call-start
  60.5 38.4 %all-gather.2.cloned.1.call-done = bf16[2,512,512]{2,1,0:T(8,128)(2,1)} async-done(((bf16[2,16,512]{2,1,0:T(8,128)(2,1)}), bf16[2,512,512]{2,1,0:T(8,128)(2,1)}) %all-gather.2.cloned.1.call-update) | async-done | bytes 1048592 | tf_op jit(solution)/shard_map/all_gather | solution.py:19
  98.9 0.0 copy-done.3
  98.9 3.5 %convolution_bitcast_fusion.1 = f32[1,512,512]{2,1,0:T(8,128)} fusion(bf16[2,512,512]{2,1,0:T(8,128)(2,1)} %all-gather.2.cloned.1.call-done, bf16[2,1,512,512]{3,2,1,0:T(8,128)(2,1)S(1)} %copy-done, bf16[2,1,512,512]{3,2,1,0:T(8,128)(2,1)S(1)} %copy-done.3), kind=kOutput, calls=%fused_computation.9 | convolution fusion | flops 1074266112 | bytes 4194304 | tf_op jit(solution)/shard_map/tsij,tsil->sjl/dot_general | solution.py:37
  102.5 0.0 reduce-scatter.5.cloned.1.call-update
  102.5 2.0 fusion.1
  104.5 0.0 copy-start.1
  104.5 1.3 copy.12
  105.8 0.0 copy-done.1
  105.8 2.3 fusion.2
  108.1 1.3 copy.13
  109.5 119.1 %reduce-scatter.3.cloned.1.call-done = f32[2,16,512]{2,1,0:T(8,128)} async-done(((f32[2,512,512]{2,1,0:T(8,128)}), f32[2,16,512]{2,1,0:T(8,128)}) %reduce-scatter.3.cloned.1.call-update) | async-done | bytes 65552 | tf_op jit(solution)/shard_map/reduce_scatter | solution.py:40
  228.6 1.6 fusion.6
  230.2 76.5 %reduce-scatter.5.cloned.1.call-done = f32[1,32,512]{2,1,0:T(8,128)} async-done(((f32[1,512,512]{2,1,0:T(8,128)}), f32[1,32,512]{2,1,0:T(8,128)}) %reduce-scatter.5.cloned.1.call-update) | async-done | bytes 65552 | tf_op jit(solution)/shard_map/reduce_scatter | solution.py:41
  306.7 1.0 fusion.19
  307.6 1.6 convert_multiply_fusion
  (4 shorter events, 0.0 us)
Async XLA Ops:
  7.2 51.2 %copy-start = (bf16[2,1,512,512]{3,2,1,0:T(8,128)(2,1)S(1)}, bf16[2,1,512,512]{3,2,1,0:T(8,128)(2,1)}, u32[]{:S(2)}) copy-start(bf16[2,1,512,512]{3,2,1,0:T(8,128)(2,1)} %param.5) | copy-start | bytes 3145732
  7.2 91.8 %all-gather.2.cloned.1.call-start = ((), (), s32[]{:S(2)}) async-start(), calls=%async_computation.2 | async-start | bytes 1081344 | tf_op jit(solution)/shard_map/all_gather | solution.py:19
  10.6 218.0 %reduce-scatter.3.cloned.1.call-start = ((), (), s32[]{:S(2)}) async-start(), calls=%async_computation.3 | async-start | bytes 2162688 | tf_op jit(solution)/shard_map/reduce_scatter | solution.py:40
  55.6 0.8 copy-start.2
  60.4 38.5 %copy-start.3 = (bf16[2,1,512,512]{3,2,1,0:T(8,128)(2,1)S(1)}, bf16[2,1,512,512]{3,2,1,0:T(8,128)(2,1)}, u32[]{:S(2)}) copy-start(bf16[2,1,512,512]{3,2,1,0:T(8,128)(2,1)} %param.4) | copy-start | bytes 3145732
  60.5 246.2 %reduce-scatter.5.cloned.1.call-start = ((), (), s32[]{:S(2)}) async-start(), calls=%async_computation.4 | async-start | bytes 1114112 | tf_op jit(solution)/shard_map/reduce_scatter | solution.py:41
  104.5 1.3 copy-start.1
Sparse Core Ops, SparseCore 0:
  12.0 86.9 all-gather.1
  103.7 124.8 reduce-scatter.2
  231.4 75.2 reduce-scatter.4
where the time goes:
time: 316 us
  waiting for transfers between devices  234 us (74%)
  blocking collectives  42.3 us (13%)
  between operations  13.8 us (4%)
  matrix products  11.8 us (4%)
  other arithmetic  10.2 us (3%)
  local copies, waits for them, and re-layouts  3.46 us (1%)
    reduce_scatter x1, waiting for transfers between devices, body(): lax.psum_scatter(dprob_tgt, 'sup', scatter_dimension=1, tiled=True)  119 us
    reduce_scatter x1, waiting for transfers between devices, body(): lax.psum_scatter(dprob_sup, 'tgt', scatter_dimension=1, tiled=True)  76.5 us
    all_gather x1, blocking collectives, body(): lax.all_gather(softmax_rows(self_sup), 'tgt', axis=1, tiled=True)  42.3 us
    all_gather x1, waiting for transfers between devices, body(): lax.all_gather(softmax_rows(self_tgt), 'sup', axis=1, tiled=True)  38.4 us
  transfers between devices with their start and end apart: 3, of which 3 were waited for; matrix products, arithmetic and copies ran while one was open for 6% of the time, Pallas kernels for 0%

commit v1 on v0

v1 whole, which is shorter than its diff:
```python
import jax
import jax.numpy as jnp
from jax import lax
from jax.experimental import pallas as pl
from jax.experimental.pallas import tpu as pltpu
from jax.sharding import PartitionSpec as P

MESH = pl.DeviceIdType.MESH
F32 = jnp.float32
BF16 = jnp.bfloat16
L = 512
RING = 8


def softmax_rows(scores):
    scores = scores.astype(F32)
    e = jnp.exp(scores - jnp.max(scores, axis=-1, keepdims=True))
    return (e / jnp.sum(e, axis=-1, keepdims=True)).astype(BF16)


def soft_back(probs, dprobs):
    weights = probs.astype(F32)
    return weights * (dprobs - jnp.sum(dprobs * weights, axis=-1, keepdims=True))


def nn(a, b):
    return lax.dot_general(a, b, (((1,), (0,)), ((), ())), preferred_element_type=F32)


def nt(a, b):
    return lax.dot_general(a, b, (((1,), (1,)), ((), ())), preferred_element_type=F32)


def tn(a, b):
    return lax.dot_general(a, b, (((0,), (0,)), ((), ())), preferred_element_type=F32)


def hops(chunk, sign):
    return 4 if (chunk == 0) == (sign == 1) else 3


def kernel(
    cross_hbm, cot_hbm, tgt_ref, sup_ref,
    out_hbm, gcross_hbm, gtgt_ref, gsup_ref,
    cross, cot, pbuf, qbuf, mix, held, left, outv, gcv,
    dpart, dcore, epart, dstage, drecv, estage, erecv, dlast, elast,
    load_sem, store_sem,
    px_s, px_r, qx_s, qx_r, pr_s, pr_r, qr_s, qr_r, pc_s, pc_r,
    dc_s, dc_r, dr_s, dr_r, er_s, er_r, dx_s, dx_r, ex_s, ex_r,
):
    t_id = lax.axis_index("tgt")
    s_id = lax.axis_index("sup")
    z, x_lo = t_id // 2, t_id % 2
    y, x_hi, core = s_id // 4, (s_id // 2) % 2, s_id % 2

    def at_y(dy, xh=None, c=None):
        xh = x_hi if xh is None else xh
        c = core if c is None else c
        return (t_id, ((y + dy + RING) % RING) * 4 + xh * 2 + c)

    def at_z(dz, xl=None):
        xl = x_lo if xl is None else xl
        return (((z + dz + RING) % RING) * 2 + xl, s_id)

    loads = [
        pltpu.make_async_copy(cross_hbm, cross, load_sem.at[0]),
        pltpu.make_async_copy(cot_hbm, cot, load_sem.at[1]),
    ]
    for c in loads:
        c.start()

    barrier = pltpu.get_barrier_semaphore()
    near = [at_y(1), at_y(-1), at_y(0, xh=1 - x_hi), at_y(0, c=1 - core), at_z(1), at_z(-1), at_z(0, xl=1 - x_lo)]
    for device in near:
        pl.semaphore_signal(barrier, inc=1, device_id=device, device_id_type=MESH)

    p_own = softmax_rows(tgt_ref[...])
    q_own = softmax_rows(sup_ref[0])
    pbuf[s_id] = p_own
    qbuf[t_id] = q_own
    pl.semaphore_wait(barrier, 7)

    pending = []

    def send(src, dst, ssem, rsem, device):
        copy = pltpu.make_async_remote_copy(
            src_ref=src, dst_ref=dst, send_sem=ssem, recv_sem=rsem, device_id=device, device_id_type=MESH
        )
        copy.start()
        pending.append(copy)
        return copy

    def p_slot(dy, chunk):
        xh = x_hi if chunk == 0 else 1 - x_hi
        return ((y + dy + RING) % RING) * 4 + xh * 2 + core

    def q_slot(dz, chunk):
        xl = x_lo if chunk == 0 else 1 - x_lo
        return ((z + dz + RING) % RING) * 2 + xl

    def sems(ssem, rsem, chunk, sign, k):
        i = (chunk * 2 + (sign == 1)) * 4 + k
        return ssem.at[i], rsem.at[i]

    p_copies, q_copies, c_copies = {}, {}, []

    def q_ring(chunk, sign, k):
        slot = q_slot(-sign * k, chunk)
        ss, rs = sems(qr_s, qr_r, chunk, sign, k)
        q_copies[chunk, sign, k] = send(qbuf.at[slot], qbuf.at[slot], ss, rs, at_z(sign))

    def p_ring(chunk, sign, k):
        slot = p_slot(-sign * k, chunk)
        ss, rs = sems(pr_s, pr_r, chunk, sign, k)
        p_copies[chunk, sign, k] = send(pbuf.at[slot], pbuf.at[slot], ss, rs, at_y(sign))

    def p_core(dy, chunk):
        slot = p_slot(dy, chunk)
        i = len(c_copies)
        c_copies.append(send(pbuf.at[slot], pbuf.at[slot], pc_s.at[i], pc_r.at[i], at_y(0, c=1 - core)))

    qx = send(qbuf.at[t_id], qbuf.at[t_id], qx_s, qx_r, at_z(0, xl=1 - x_lo))
    px = send(pbuf.at[s_id], pbuf.at[s_id], px_s, px_r, at_y(0, xh=1 - x_hi))
    for sign in (1, -1):
        q_ring(0, sign, 0)
        p_ring(0, sign, 0)
    p_core(0, 0)

    for c in loads:
        c.wait()

    qx.wait_recv()
    for sign in (1, -1):
        q_ring(1, sign, 0)
    px.wait_recv()
    for sign in (1, -1):
        p_ring(1, sign, 0)
    p_core(0, 1)

    for k in range(4):
        for chunk in (0, 1):
            for sign in (1, -1):
                if k < hops(chunk, sign):
                    q_copies[chunk, sign, k].wait_recv()
                    if k + 1 < hops(chunk, sign):
                        q_ring(chunk, sign, k + 1)
            for sign in (1, -1):
                if k < hops(chunk, sign):
                    p_copies[chunk, sign, k].wait_recv()
                    if k + 1 < hops(chunk, sign):
                        p_ring(chunk, sign, k + 1)
                    p_core(-sign * (k + 1), chunk)

    q_all = qbuf[...].reshape(L, L)
    for t in range(2):
        mix[t] = nt(cross[t, 0], q_all).astype(BF16)
    for t in range(2):
        d = nt(cot[t, 0], mix[t]).astype(BF16)
        for s in range(32):
            dpart[s % 2, s // 4, (s // 2) % 2, t] = d[s * 16:(s + 1) * 16]

    order = (4, -3, 3, -2, 2, -1, 1, 0)
    d_core = {}
    for i, dy in enumerate(order):
        dest = (y + dy + RING) % RING
        d_core[dy % RING] = send(
            dpart.at[1 - core, dest], dcore.at[dest], dc_s.at[i], dc_r.at[i], at_y(0, c=1 - core)
        )

    for c in c_copies:
        c.wait_recv()
    for t in range(2):
        p_t = pbuf[:, t].reshape(L, L)
        left[t] = nn(p_t, cross[t, 0]).astype(BF16)
    e = tn(cot[0, 0], left[0]) + tn(cot[1, 0], left[1])
    epart[...] = e.astype(BF16).reshape(16, 32, L)

    def d_local(dy, chunk):
        dest = (y + dy + RING) % RING
        xh = x_hi if chunk == 0 else 1 - x_hi
        if dy % RING in d_core:
            d_core.pop(dy % RING).wait_recv()
        return dpart[core, dest, xh].astype(F32) + dcore[dest, xh].astype(F32)

    def e_local(dz, chunk):
        return epart[q_slot(dz, chunk)].astype(F32)

    d_copies, e_copies = {}, {}

    def d_ring(chunk, sign, k):
        n = hops(chunk, sign)
        i = (chunk * 2 + (sign == 1)) * 4 + k
        total = d_local(sign * (n - k), chunk)
        if k:
            total += drecv[i - 1].astype(F32)
        dstage[i] = total.astype(BF16)
        d_copies[chunk, sign, k] = send(dstage.at[i], drecv.at[i], dr_s.at[i], dr_r.at[i], at_y(sign))

    def e_ring(chunk, sign, k):
        n = hops(chunk, sign)
        i = (chunk * 2 + (sign == 1)) * 4 + k
        total = e_local(sign * (n - k), chunk)
        if k:
            total += erecv[i - 1].astype(F32)
        estage[i] = total.astype(BF16)
        e_copies[chunk, sign, k] = send(estage.at[i], erecv.at[i], er_s.at[i], er_r.at[i], at_z(sign))

    stores = []

    def work(i):
        t = i % 2
        if i < 2:
            outv[t, 0] = nn(pbuf[:, t].reshape(L, L), mix[t]).astype(BF16)
            stores.append(pltpu.make_async_copy(outv.at[t], out_hbm.at[t], store_sem.at[t]))
            stores[-1].start()
        elif i < 4:
            held[t] = nn(cot[t, 0], qbuf[...].reshape(L, L)).astype(BF16)
        elif i < 6:
            gcv[t, 0] = tn(pbuf[:, t].reshape(L, L), held[t]).astype(BF16)
            stores.append(pltpu.make_async_copy(gcv.at[t], gcross_hbm.at[t], store_sem.at[2 + t]))
            stores[-1].start()

    for k in range(4):
        for chunk in (1, 0):
            for sign in (1, -1):
                if k < hops(chunk, sign):
                    if k:
                        d_copies[chunk, sign, k - 1].wait_recv()
                    d_ring(chunk, sign, k)
            for sign in (1, -1):
                if k < hops(chunk, sign):
                    if k:
                        e_copies[chunk, sign, k - 1].wait_recv()
                    e_ring(chunk, sign, k)
        work(2 * k)
        work(2 * k + 1)

    def d_final(chunk):
        total = d_local(0, chunk)
        for sign in (1, -1):
            n = hops(chunk, sign)
            d_copies[chunk, sign, n - 1].wait_recv()
            total += drecv[(chunk * 2 + (sign == 1)) * 4 + n - 1].astype(F32)
        return total

    def e_final(chunk):
        total = e_local(0, chunk)
        for sign in (1, -1):
            n = hops(chunk, sign)
            e_copies[chunk, sign, n - 1].wait_recv()
            total += erecv[(chunk * 2 + (sign == 1)) * 4 + n - 1].astype(F32)
        return total

    dlast[0] = d_final(1).astype(BF16)
    dx = send(dlast.at[0], dlast.at[1], dx_s, dx_r, at_y(0, xh=1 - x_hi))
    elast[0] = e_final(1).astype(BF16)
    ex = send(elast.at[0], elast.at[1], ex_s, ex_r, at_z(0, xl=1 - x_lo))
    d_own = d_final(0)
    e_own = e_final(0)
    ex.wait_recv()
    gsup_ref[0] = soft_back(qbuf[t_id], e_own + elast[1].astype(F32))
    dx.wait_recv()
    gtgt_ref[...] = soft_back(pbuf[s_id], d_own + dlast[1].astype(F32))

    for copy in pending:
        copy.wait_send()
    for copy in stores:
        copy.wait()


def body(cross_kernel, cotangent, self_tgt, self_sup):
    vmem, dma = pltpu.VMEM, pltpu.SemaphoreType.DMA
    any_spec = pl.BlockSpec(memory_space=pl.ANY)
    vmem_spec = pl.BlockSpec(memory_space=pltpu.VMEM)
    docs = (2, 1, L, L)
    return pl.pallas_call(
        kernel,
        out_shape=(
            jax.ShapeDtypeStruct(docs, BF16),
            jax.ShapeDtypeStruct(docs, BF16),
            jax.ShapeDtypeStruct((2, 16, L), F32),
            jax.ShapeDtypeStruct((1, 32, L), F32),
        ),
        in_specs=[any_spec, any_spec, vmem_spec, vmem_spec],
        out_specs=(any_spec, any_spec, vmem_spec, vmem_spec),
        scratch_shapes=[
            vmem(docs, BF16), vmem(docs, BF16),
            vmem((32, 2, 16, L), BF16), vmem((16, 32, L), BF16),
            vmem((2, L, L), BF16), vmem((2, L, L), BF16), vmem((2, L, L), BF16),
            vmem(docs, BF16), vmem(docs, BF16),
            vmem((2, 8, 2, 2, 16, L), BF16), vmem((8, 2, 2, 16, L), BF16), vmem((16, 32, L), BF16),
            vmem((16, 2, 16, L), BF16), vmem((16, 2, 16, L), BF16),
            vmem((16, 32, L), BF16), vmem((16, 32, L), BF16),
            vmem((2, 2, 16, L), BF16), vmem((2, 32, L), BF16),
            dma((2,)), dma((4,)),
            dma, dma, dma, dma, dma((16,)), dma((16,)), dma((16,)), dma((16,)), dma((16,)), dma((16,)),
            dma((8,)), dma((8,)), dma((16,)), dma((16,)), dma((16,)), dma((16,)), dma, dma, dma, dma,
        ],
        compiler_params=pltpu.CompilerParams(
            collective_id=0, has_side_effects=True, vmem_limit_bytes=48 * 1024 * 1024
        ),
        name="layer",
    )(cross_kernel, cotangent, self_tgt, self_sup)


def solution(mesh):
    in_specs = (
        P("tgt", "sup", None, None),
        P("tgt", "sup", None, None),
        P("tgt", "sup", None),
        P("sup", "tgt", None),
    )
    out_specs = (
        P("tgt", "sup", None, None),
        P("tgt", "sup", None, None),
        P("tgt", "sup", None),
        P("sup", "tgt", None),
    )
    return jax.shard_map(body, mesh=mesh, in_specs=in_specs, out_specs=out_specs, check_vma=False)
```

time: 316 us -> 59.3 us (0.19)
  waiting for transfers between devices: 234 us -> 0 us
  Pallas kernels: 0 us -> 51.2 us
  blocking collectives: 42.3 us -> 0 us
  between operations: 13.8 us -> 0.65 us
  matrix products: 11.8 us -> 0 us
  other arithmetic: 10.2 us -> 0 us
  local copies, waits for them, and re-layouts: 3.46 us -> 7.16 us
    reduce_scatter x2 -> x0, waiting for transfers between devices: 196 us -> none  [the longest x1 119 us: body(): lax.psum_scatter(dprob_tgt, 'sup', scatter_dimension=1, tiled=True)]
    pallas_call x0 -> x1, Pallas kernels: none -> 51.2 us  [body(): pl.pallas_call(kernel, out_shape=(jax.ShapeDtypeStruct(docs, BF16), jax.S...]
    all_gather x1 -> x0, blocking collectives: 42.3 us -> none  [body(): lax.all_gather(softmax_rows(self_sup), 'tgt', axis=1, tiled=True)]
    all_gather x1 -> x0, waiting for transfers between devices: 38.4 us -> none  [body(): lax.all_gather(softmax_rows(self_tgt), 'sup', axis=1, tiled=True)]
    dot_general x5 -> x0, matrix products: 11.8 us -> none  [the longest x1 3.5 us: body(): jnp.einsum('tsij,tsil->sjl', cotangent, left_side, preferred_element_type...]
    unnamed x10 -> x12, local copies, waits for them, and re-layouts: 3.46 us -> 7.16 us
  transfers between devices with their start and end apart: 3 -> 0, of which waited for: 3 -> 0; matrix products, arithmetic and copies ran while one was open for 6% -> 0% of each run, Pallas kernels for 0% -> 0%
where the time goes in v1:
time: 59.3 us; the launch traced here: 59 us
  Pallas kernels  51.2 us (86%)
  local copies, waits for them, and re-layouts  7.16 us (12%)
  between operations  0.65 us (1%)
    pallas_call x1, Pallas kernels, body(): pl.pallas_call(kernel, out_shape=(jax.ShapeDtypeStruct(docs, BF16), jax.S...  51.2 us
    unnamed x12, local copies, waits for them, and re-layouts  7.16 us

profile of v1, /device:TPU:8, one launch (start us, length us, event | category | flops | bytes accessed | tf_op | source)
XLA Modules:
  0.0 59.0 jit_solution(16423061696132527161)
XLA Ops:
  0.6 0.0 copy-start
  0.6 1.2 %copy-done = bf16[2,1,512,512]{3,2,1,0:T(8,128)(2,1)S(1)} copy-done((bf16[2,1,512,512]{3,2,1,0:T(8,128)(2,1)S(1)}, bf16[2,1,512,512]{3,2,1,0:T(8,128)(2,1)}, u32[]{:S(2)}) %copy-start) | copy-done | bytes 1048600
  1.9 0.0 copy-start.1
  1.9 1.2 %copy-done.1 = bf16[2,1,512,512]{3,2,1,0:T(8,128)(2,1)S(1)} copy-done((bf16[2,1,512,512]{3,2,1,0:T(8,128)(2,1)S(1)}, bf16[2,1,512,512]{3,2,1,0:T(8,128)(2,1)}, u32[]{:S(2)}) %copy-start.1) | copy-done | bytes 1048600
  3.1 0.0 copy-start.2
  3.1 0.8 %copy-done.2 = bf16[2,16,512]{2,1,0:T(8,128)(2,1)S(1)} copy-done((bf16[2,16,512]{2,1,0:T(8,128)(2,1)S(1)}, bf16[2,16,512]{2,1,0:T(8,128)(2,1)}, u32[]{:S(2)}) %copy-start.2) | copy-done | bytes 32792
  3.8 0.0 copy-start.3
  3.8 0.8 %copy-done.3 = bf16[1,32,512]{2,1,0:T(8,128)(2,1)S(1)} copy-done((bf16[1,32,512]{2,1,0:T(8,128)(2,1)S(1)}, bf16[1,32,512]{2,1,0:T(8,128)(2,1)}, u32[]{:S(2)}) %copy-start.3) | copy-done | bytes 32792
  4.6 51.2 %layer.1 = (bf16[2,1,512,512]{3,2,1,0:T(8,128)(2,1)S(1)}, bf16[2,1,512,512]{3,2,1,0:T(8,128)(2,1)S(1)}, f32[2,16,512]{2,1,0:T(8,128)S(1)}, f32[1,32,512]{2,1,0:T(8,128)S(1)}) custom-call(bf16[2,1,512,512]{3,2,1,0:T(8,128)(2,1)S(1)} %copy-done, bf16[2,1,512,512]{3,2,1,0:T(8,128)(2,1)S(1)} %copy-done.1, bf16[2,16,512]{2,1,0:T(8,128)(2,1)S(1)} %copy-done.2, ...), custom_call_target="tpu_custom_call" | custom-call | tf_op jit(solution)/shard_map/layer/pallas_call | solution.py:276
  55.8 1.0 %copy.12 = bf16[2,1,512,512]{3,2,1,0:T(8,128)(2,1)} copy(bf16[2,1,512,512]{3,2,1,0:T(8,128)(2,1)S(1)} %get-tuple-element.8) | data formatting | bytes 2097152
  56.8 1.0 %copy.13 = bf16[2,1,512,512]{3,2,1,0:T(8,128)(2,1)} copy(bf16[2,1,512,512]{3,2,1,0:T(8,128)(2,1)S(1)} %get-tuple-element.9) | data formatting | bytes 2097152
  57.7 0.6 %copy.14 = f32[2,16,512]{2,1,0:T(8,128)} copy(f32[2,16,512]{2,1,0:T(8,128)S(1)} %get-tuple-element.10) | data formatting | bytes 131072
  58.4 0.6 %copy.15 = f32[1,32,512]{2,1,0:T(8,128)} copy(f32[1,32,512]{2,1,0:T(8,128)S(1)} %get-tuple-element.11) | data formatting | bytes 131072
Async XLA Ops:
  0.6 1.2 %copy-start = (bf16[2,1,512,512]{3,2,1,0:T(8,128)(2,1)S(1)}, bf16[2,1,512,512]{3,2,1,0:T(8,128)(2,1)}, u32[]{:S(2)}) copy-start(bf16[2,1,512,512]{3,2,1,0:T(8,128)(2,1)} %cross_hbm.1) | copy-start | bytes 3145732
  1.9 1.2 %copy-start.1 = (bf16[2,1,512,512]{3,2,1,0:T(8,128)(2,1)S(1)}, bf16[2,1,512,512]{3,2,1,0:T(8,128)(2,1)}, u32[]{:S(2)}) copy-start(bf16[2,1,512,512]{3,2,1,0:T(8,128)(2,1)} %cot_hbm.1) | copy-start | bytes 3145732
  3.1 0.8 %copy-start.2 = (bf16[2,16,512]{2,1,0:T(8,128)(2,1)S(1)}, bf16[2,16,512]{2,1,0:T(8,128)(2,1)}, u32[]{:S(2)}) copy-start(bf16[2,16,512]{2,1,0:T(8,128)(2,1)} %tgt_ref.1) | copy-start | bytes 98308
  3.8 0.8 %copy-start.3 = (bf16[1,32,512]{2,1,0:T(8,128)(2,1)S(1)}, bf16[1,32,512]{2,1,0:T(8,128)(2,1)}, u32[]{:S(2)}) copy-start(bf16[1,32,512]{2,1,0:T(8,128)(2,1)} %sup_ref.1) | copy-start | bytes 98308

commit v2 on v1

--- a/solution.py
+++ b/solution.py
@@ -40,11 +40,11 @@
 
 
 def kernel(
-    cross_hbm, cot_hbm, tgt_ref, sup_ref,
-    out_hbm, gcross_hbm, gtgt_ref, gsup_ref,
-    cross, cot, pbuf, qbuf, mix, held, left, outv, gcv,
+    cross_hbm, cot_hbm, tgt_hbm, sup_hbm,
+    outv, gcv, gtgt_ref, gsup_ref,
+    cross, cot, tgt_ref, sup_ref, pbuf, qbuf, mix, held, left,
     dpart, dcore, epart, dstage, drecv, estage, erecv, dlast, elast,
-    load_sem, store_sem,
+    load_sem,
     px_s, px_r, qx_s, qx_r, pr_s, pr_r, qr_s, qr_r, pc_s, pc_r,
     dc_s, dc_r, dr_s, dr_r, er_s, er_r, dx_s, dx_r, ex_s, ex_r,
 ):
@@ -63,6 +63,8 @@
         return (((z + dz + RING) % RING) * 2 + xl, s_id)
 
     loads = [
+        pltpu.make_async_copy(tgt_hbm, tgt_ref, load_sem.at[2]),
+        pltpu.make_async_copy(sup_hbm, sup_ref, load_sem.at[3]),
         pltpu.make_async_copy(cross_hbm, cross, load_sem.at[0]),
         pltpu.make_async_copy(cot_hbm, cot, load_sem.at[1]),
     ]
@@ -74,6 +76,8 @@
     for device in near:
         pl.semaphore_signal(barrier, inc=1, device_id=device, device_id_type=MESH)
 
+    loads.pop(0).wait()
+    loads.pop(0).wait()
     p_own = softmax_rows(tgt_ref[...])
     q_own = softmax_rows(sup_ref[0])
     pbuf[s_id] = p_own
@@ -205,20 +209,14 @@
         estage[i] = total.astype(BF16)
         e_copies[chunk, sign, k] = send(estage.at[i], erecv.at[i], er_s.at[i], er_r.at[i], at_z(sign))
 
-    stores = []
-
     def work(i):
         t = i % 2
         if i < 2:
             outv[t, 0] = nn(pbuf[:, t].reshape(L, L), mix[t]).astype(BF16)
-            stores.append(pltpu.make_async_copy(outv.at[t], out_hbm.at[t], store_sem.at[t]))
-            stores[-1].start()
         elif i < 4:
             held[t] = nn(cot[t, 0], qbuf[...].reshape(L, L)).astype(BF16)
         elif i < 6:
             gcv[t, 0] = tn(pbuf[:, t].reshape(L, L), held[t]).astype(BF16)
-            stores.append(pltpu.make_async_copy(gcv.at[t], gcross_hbm.at[t], store_sem.at[2 + t]))
-            stores[-1].start()
 
     for k in range(4):
         for chunk in (1, 0):
@@ -264,35 +262,41 @@
 
     for copy in pending:
         copy.wait_send()
-    for copy in stores:
+
+
+def write_out(*refs):
+    copies = [pltpu.make_async_copy(refs[i], refs[4 + i], refs[8].at[i]) for i in range(4)]
+    for copy in copies:
+        copy.start()
+    for copy in copies:
         copy.wait()
 
 
 def body(cross_kernel, cotangent, self_tgt, self_sup):
     vmem, dma = pltpu.VMEM, pltpu.SemaphoreType.DMA
-    any_spec = pl.BlockSpec(memory_space=pl.ANY)
+    hbm_spec = pl.BlockSpec(memory_space=pltpu.HBM)
     vmem_spec = pl.BlockSpec(memory_space=pltpu.VMEM)
     docs = (2, 1, L, L)
-    return pl.pallas_call(
+    outs = (
+        jax.ShapeDtypeStruct(docs, BF16),
+        jax.ShapeDtypeStruct(docs, BF16),
+        jax.ShapeDtypeStruct((2, 16, L), F32),
+        jax.ShapeDtypeStruct((1, 32, L), F32),
+    )
+    results = pl.pallas_call(
         kernel,
-        out_shape=(
-            jax.ShapeDtypeStruct(docs, BF16),
-            jax.ShapeDtypeStruct(docs, BF16),
-            jax.ShapeDtypeStruct((2, 16, L), F32),
-            jax.ShapeDtypeStruct((1, 32, L), F32),
-        ),
-        in_specs=[any_spec, any_spec, vmem_spec, vmem_spec],
-        out_specs=(any_spec, any_spec, vmem_spec, vmem_spec),
+        out_shape=outs,
+        in_specs=[hbm_spec] * 4,
+        out_specs=(vmem_spec,) * 4,
         scratch_shapes=[
-            vmem(docs, BF16), vmem(docs, BF16),
+            vmem(docs, BF16), vmem(docs, BF16), vmem((2, 16, L), BF16), vmem((1, 32, L), BF16),
             vmem((32, 2, 16, L), BF16), vmem((16, 32, L), BF16),
             vmem((2, L, L), BF16), vmem((2, L, L), BF16), vmem((2, L, L), BF16),
-            vmem(docs, BF16), vmem(docs, BF16),
             vmem((2, 8, 2, 2, 16, L), BF16), vmem((8, 2, 2, 16, L), BF16), vmem((16, 32, L), BF16),
             vmem((16, 2, 16, L), BF16), vmem((16, 2, 16, L), BF16),
             vmem((16, 32, L), BF16), vmem((16, 32, L), BF16),
             vmem((2, 2, 16, L), BF16), vmem((2, 32, L), BF16),
-            dma((2,)), dma((4,)),
+            dma((4,)),
             dma, dma, dma, dma, dma((16,)), dma((16,)), dma((16,)), dma((16,)), dma((16,)), dma((16,)),
             dma((8,)), dma((8,)), dma((16,)), dma((16,)), dma((16,)), dma((16,)), dma, dma, dma, dma,
         ],
@@ -300,7 +304,16 @@
             collective_id=0, has_side_effects=True, vmem_limit_bytes=48 * 1024 * 1024
         ),
         name="layer",
-    )(cross_kernel, cotangent, self_tgt, self_sup)
+    )(*[pltpu.with_memory_space_constraint(x, pltpu.HBM) for x in (cross_kernel, cotangent, self_tgt, self_sup)])
+    return pl.pallas_call(
+        write_out,
+        out_shape=outs,
+        in_specs=[vmem_spec] * 4,
+        out_specs=(hbm_spec,) * 4,
+        scratch_shapes=[dma((4,))],
+        compiler_params=pltpu.CompilerParams(vmem_limit_bytes=1024 * 1024),
+        name="write_out",
+    )(*results)
 
 
 def solution(mesh):

time: 59.3 us -> 53.2 us (0.90)
  local copies, waits for them, and re-layouts: 7.16 us -> 0 us
  Pallas kernels: 51.2 us -> 52.4 us
    unnamed x12 -> x0, local copies, waits for them, and re-layouts: 7.16 us -> none
    pallas_call x1 -> x2, Pallas kernels: 51.2 us -> 52.4 us  [the longest x1 51 us: body(): pl.pallas_call(kernel, out_shape=outs, in_specs=[hbm_spec] * 4, out_specs...]
where the time goes in v2:
time: 53.2 us; the launch traced here: 53 us
  Pallas kernels  52.4 us (98%)
  between operations  0.64 us (1%)
    pallas_call x1, Pallas kernels, body(): pl.pallas_call(kernel, out_shape=outs, in_specs=[hbm_spec] * 4, out_specs...  51 us
    pallas_call x1, Pallas kernels, body(): pl.pallas_call(write_out, out_shape=outs, in_specs=[vmem_spec] * 4, out_s...  1.38 us

profile of v2, /device:TPU:8, one launch (start us, length us, event | category | flops | bytes accessed | tf_op | source)
XLA Modules:
  0.0 53.0 jit_solution(15322465543538126838)
XLA Ops:
  0.6 51.0 %layer.1 = (bf16[2,1,512,512]{3,2,1,0:T(8,128)(2,1)S(1)}, bf16[2,1,512,512]{3,2,1,0:T(8,128)(2,1)S(1)}, f32[2,16,512]{2,1,0:T(8,128)S(1)}, f32[1,32,512]{2,1,0:T(8,128)S(1)}) custom-call(bf16[2,1,512,512]{3,2,1,0:T(8,128)(2,1)} %cross_hbm.1, bf16[2,1,512,512]{3,2,1,0:T(8,128)(2,1)} %cot_hbm.1, bf16[2,16,512]{2,1,0:T(8,128)(2,1)} %tgt_hbm.1, ...), custom_call_target="tpu_custom_call" | custom-call | tf_op jit(solution)/shard_map/layer/pallas_call | solution.py:286
  51.7 1.4 %write_out.1 = (bf16[2,1,512,512]{3,2,1,0:T(8,128)(2,1)}, bf16[2,1,512,512]{3,2,1,0:T(8,128)(2,1)}, f32[2,16,512]{2,1,0:T(8,128)}, f32[1,32,512]{2,1,0:T(8,128)}) custom-call(bf16[2,1,512,512]{3,2,1,0:T(8,128)(2,1)S(1)} %get-tuple-element.8.refs_0_, bf16[2,1,512,512]{3,2,1,0:T(8,128)(2,1)S(1)} %get-tuple-element.9.refs_1_, ...), custom_call_target="tpu_custom_call" | custom-call | tf_op jit(solution)/shard_map/write_out/pallas_call | solution.py:308

commit v3 on v2

v3 whole, which is shorter than its diff:
```python
import jax
import jax.numpy as jnp
from jax import lax
from jax.experimental import pallas as pl
from jax.experimental.pallas import tpu as pltpu
from jax.sharding import PartitionSpec as P

MESH = pl.DeviceIdType.MESH
F32 = jnp.float32
BF16 = jnp.bfloat16
L = 512
RING = 8


def softmax_rows(scores):
    scores = scores.astype(F32)
    e = jnp.exp(scores - jnp.max(scores, axis=-1, keepdims=True))
    return (e / jnp.sum(e, axis=-1, keepdims=True)).astype(BF16)


def soft_back(probs, dprobs):
    weights = probs.astype(F32)
    return weights * (dprobs - jnp.sum(dprobs * weights, axis=-1, keepdims=True))


def nn(a, b):
    return lax.dot_general(a, b, (((1,), (0,)), ((), ())), preferred_element_type=F32)


def nt(a, b):
    return lax.dot_general(a, b, (((1,), (1,)), ((), ())), preferred_element_type=F32)


def tn(a, b):
    return lax.dot_general(a, b, (((0,), (0,)), ((), ())), preferred_element_type=F32)


def kernel(
    cross_hbm, cot_hbm, tgt_hbm, sup_hbm,
    outv, gcv, gtgt_ref, gsup_ref,
    cross, cot, tgt_ref, sup_ref, pbuf, qbuf, mix, held, left,
    dpart, dcore, epart, ecross, dstage, drecv, estage, erecv, dlast,
    load_sem,
    px_s, px_r, qx_s, qx_r, pr_s, pr_r, qr_s, qr_r, pc_s, pc_r,
    dc_s, dc_r, dr_s, dr_r, er_s, er_r, dx_s, dx_r, ex_s, ex_r,
):
    t_id = lax.axis_index("tgt")
    s_id = lax.axis_index("sup")
    z, x_lo = t_id // 2, t_id % 2
    y, x_hi, core = s_id // 4, (s_id // 2) % 2, s_id % 2

    def at_y(dy, xh=None, c=None):
        xh = x_hi if xh is None else xh
        c = core if c is None else c
        return (t_id, ((y + dy + RING) % RING) * 4 + xh * 2 + c)

    def at_z(dz, xl=None):
        xl = x_lo if xl is None else xl
        return (((z + dz + RING) % RING) * 2 + xl, s_id)

    loads = [
        pltpu.make_async_copy(tgt_hbm, tgt_ref, load_sem.at[2]),
        pltpu.make_async_copy(sup_hbm, sup_ref, load_sem.at[3]),
        pltpu.make_async_copy(cross_hbm, cross, load_sem.at[0]),
        pltpu.make_async_copy(cot_hbm, cot, load_sem.at[1]),
    ]
    for c in loads:
        c.start()

    barrier = pltpu.get_barrier_semaphore()
    near = [at_y(0, xh=1 - x_hi), at_y(0, c=1 - core), at_z(0, xl=1 - x_lo)]
    near += [at(step) for at in (at_y, at_z) for step in (2, -2, 1, -1)]
    for device in near:
        pl.semaphore_signal(barrier, inc=1, device_id=device, device_id_type=MESH)

    loads.pop(0).wait()
    loads.pop(0).wait()
    p_own = softmax_rows(tgt_ref[...])
    q_own = softmax_rows(sup_ref[0])
    pbuf[s_id] = p_own
    qbuf[t_id] = q_own
    pl.semaphore_wait(barrier, len(near))

    pending = []

    def send(src, dst, ssem, rsem, device):
        copy = pltpu.make_async_remote_copy(
            src_ref=src, dst_ref=dst, send_sem=ssem, recv_sem=rsem, device_id=device, device_id_type=MESH
        )
        copy.start()
        pending.append(copy)
        return copy

    def p_slot(dy, chunk):
        xh = x_hi if chunk == 0 else 1 - x_hi
        return ((y + dy + RING) % RING) * 4 + xh * 2 + core

    def q_slot(dz, chunk=0):
        xl = x_lo if chunk == 0 else 1 - x_lo
        return ((z + dz + RING) % RING) * 2 + xl

    def place(chunk, origin, half=0):
        return chunk * 9 + (origin + 3 if origin != 4 else 7 + half)

    c_copies = []

    def p_send(chunk, origin, step):
        slot = p_slot(origin, chunk)
        i = place(chunk, origin - step)
        return send(pbuf.at[slot], pbuf.at[slot], pr_s.at[i], pr_r.at[i], at_y(step))

    def p_half(chunk, sign):
        slot = p_slot(-2 * sign, chunk)
        h = (1 - sign) // 2
        i = place(chunk, 4, h)
        return send(pbuf.at[slot, h], pbuf.at[slot, h], pr_s.at[i], pr_r.at[i], at_y(2 * sign))

    def q_send(origin, step):
        slot = q_slot(origin)
        i = place(0, origin - step)
        return send(qbuf.at[slot], qbuf.at[slot], qr_s.at[i], qr_r.at[i], at_z(step))

    def q_half(sign):
        slot = q_slot(-2 * sign)
        h = (1 - sign) // 2
        i = place(0, 4, h)
        rows = pl.ds(h * 16, 16)
        return send(qbuf.at[slot, rows], qbuf.at[slot, rows], qr_s.at[i], qr_r.at[i], at_z(2 * sign))

    def q_cross(dz):
        slot = q_slot(dz)
        i = dz + 3
        return send(qbuf.at[slot], qbuf.at[slot], qx_s.at[i], qx_r.at[i], at_z(0, xl=1 - x_lo))

    def p_core(dy, chunk):
        slot = p_slot(dy, chunk)
        i = len(c_copies)
        c_copies.append(send(pbuf.at[slot], pbuf.at[slot], pc_s.at[i], pc_r.at[i], at_y(0, c=1 - core)))

    q_in, x_in, p_in = {}, [], {}
    for step in (2, -2, 1, -1):
        q_in[step] = q_send(0, step)
    x_in.append(q_cross(0))
    px = send(pbuf.at[s_id], pbuf.at[s_id], px_s, px_r, at_y(0, xh=1 - x_hi))
    for step in (2, -2, 1, -1):
        p_in[0, step] = p_send(0, 0, step)
    p_core(0, 0)

    for c in loads:
        c.wait()

    for sign in (1, -1):
        q_in[sign].wait_recv()
        x_in.append(q_cross(-sign))
    for sign in (1, -1):
        q_in[2 * sign].wait_recv()
        q_in[3 * sign] = q_send(-2 * sign, sign)
        q_in[4 * sign] = q_half(sign)
        x_in.append(q_cross(-2 * sign))
    for sign in (1, -1):
        p_in[0, sign].wait_recv()
        p_core(-sign, 0)

    def p_second(chunk):
        for sign in (1, -1):
            p_in[chunk, 2 * sign].wait_recv()
            p_in[chunk, 3 * sign] = p_send(chunk, -2 * sign, sign)
            p_in[chunk, 4 * sign] = p_half(chunk, sign)
            p_core(-2 * sign, chunk)

    def p_third(chunk):
        for sign in (1, -1):
            p_in[chunk, 3 * sign].wait_recv()
            p_core(-3 * sign, chunk)
        for sign in (1, -1):
            p_in[chunk, 4 * sign].wait_recv()
        p_core(4, chunk)

    p_second(0)
    px.wait_recv()
    for step in (2, -2, 1, -1):
        p_in[1, step] = p_send(1, 0, step)
    p_core(0, 1)
    for sign in (1, -1):
        q_in[3 * sign].wait_recv()
        x_in.append(q_cross(-3 * sign))
    for sign in (1, -1):
        q_in[4 * sign].wait_recv()
    x_in.append(q_cross(4))
    p_third(0)
    for sign in (1, -1):
        p_in[1, sign].wait_recv()
        p_core(-sign, 1)
    p_second(1)

    for c in x_in:
        c.wait_recv()
    q_all = qbuf[...].reshape(L, L)
    for t in range(2):
        mix[t] = nt(cross[t, 0], q_all).astype(BF16)
    p_third(1)
    for t in range(2):
        d = nt(cot[t, 0], mix[t]).astype(BF16)
        for s in range(32):
            dpart[s % 2, s // 4, (s // 2) % 2, t] = d[s * 16:(s + 1) * 16]

    order = (4, 3, -3, 2, -2, 1, -1, 0)
    d_in = {}
    for i, dy in enumerate(order):
        dest = (y + dy + RING) % RING
        d_in[dy] = send(
            dpart.at[1 - core, dest], dcore.at[dest], dc_s.at[i], dc_r.at[i], at_y(0, c=1 - core)
        )

    for c in c_copies:
        c.wait_recv()
    for t in range(2):
        p_t = pbuf[:, t].reshape(L, L)
        left[t] = nn(p_t, cross[t, 0]).astype(BF16)
    e = tn(cot[0, 0], left[0]) + tn(cot[1, 0], left[1])
    epart[...] = e.astype(BF16).reshape(16, 32, L)

    e_in = {}
    for i, dz in enumerate(order):
        slot = q_slot(dz, 1)
        e_in[dz] = send(epart.at[slot], ecross.at[i], ex_s.at[i], ex_r.at[i], at_z(0, xl=1 - x_lo))

    def d_local(dy, chunk):
        dest = (y + dy + RING) % RING
        xh = x_hi if chunk == 0 else 1 - x_hi
        return dpart[core, dest, xh].astype(F32) + dcore[dest, xh].astype(F32)

    def e_local(dz):
        return epart[q_slot(dz)].astype(F32) + ecross[order.index(dz)].astype(F32)

    d_out, e_out = {}, {}

    def d_send(chunk, dy, step, value):
        i = place(chunk, dy)
        dstage[i] = value.astype(BF16)
        d_out[chunk, dy] = send(dstage.at[i], drecv.at[i], dr_s.at[i], dr_r.at[i], at_y(step))

    def d_half(chunk, sign):
        h = (1 - sign) // 2
        i, j = place(chunk, 4), place(chunk, 4, h)
        d_out[chunk, 4 * sign] = send(
            dstage.at[i, h], drecv.at[i, h], dr_s.at[j], dr_r.at[j], at_y(2 * sign)
        )

    def e_send(dz, step, value):
        i = place(0, dz)
        estage[i] = value.astype(BF16)
        e_out[dz] = send(estage.at[i], erecv.at[i], er_s.at[i], er_r.at[i], at_z(step))

    def e_half(sign):
        h = (1 - sign) // 2
        i, j = place(0, 4), place(0, 4, h)
        rows = pl.ds(h * 16, 16)
        e_out[4 * sign] = send(
            estage.at[i, rows], erecv.at[i, rows], er_s.at[j], er_r.at[j], at_z(2 * sign)
        )

    def d_first(chunk):
        dstage[place(chunk, 4)] = d_local(4, chunk).astype(BF16)
        for sign in (1, -1):
            d_half(chunk, sign)
        for sign in (1, -1):
            d_send(chunk, 3 * sign, sign, d_local(3 * sign, chunk))

    def d_second(chunk):
        for sign in (1, -1):
            d_out[chunk, 3 * sign].wait_recv()
            d_out[chunk, 4 * sign].wait_recv()
            h = (1 - sign) // 2
            total = d_local(2 * sign, chunk) + drecv[place(chunk, 3 * sign)].astype(F32)
            far = drecv[place(chunk, 4), h].astype(F32)
            both = [total[0], total[1]]
            both[h] = both[h] + far
            i = place(chunk, 2 * sign)
            dstage[i, 0] = both[0].astype(BF16)
            dstage[i, 1] = both[1].astype(BF16)
            d_out[chunk, 2 * sign] = send(dstage.at[i], drecv.at[i], dr_s.at[i], dr_r.at[i], at_y(2 * sign))

    def d_third(chunk):
        for sign in (1, -1):
            d_send(chunk, sign, sign, d_local(sign, chunk))

    def e_first():
        for dz in (4, 3, -3):
            e_in[dz].wait_recv()
        estage[place(0, 4)] = e_local(4).astype(BF16)
        for sign in (1, -1):
            e_half(sign)
        for sign in (1, -1):
            e_send(3 * sign, sign, e_local(3 * sign))

    def e_second():
        for dz in (2, -2):
            e_in[dz].wait_recv()
        for sign in (1, -1):
            e_out[3 * sign].wait_recv()
            e_out[4 * sign].wait_recv()
            h = (1 - sign) // 2
            total = e_local(2 * sign) + erecv[place(0, 3 * sign)].astype(F32)
            far = erecv[place(0, 4), h * 16:(h + 1) * 16].astype(F32)
            both = [total[:16], total[16:]]
            both[h] = both[h] + far
            i = place(0, 2 * sign)
            estage[i, 0:16] = both[0].astype(BF16)
            estage[i, 16:32] = both[1].astype(BF16)
            e_out[2 * sign] = send(estage.at[i], erecv.at[i], er_s.at[i], er_r.at[i], at_z(2 * sign))

    def e_third():
        for dz in (1, -1, 0):
            e_in[dz].wait_recv()
        for sign in (1, -1):
            e_send(sign, sign, e_local(sign))

    def out_part(t):
        outv[t, 0] = nn(pbuf[:, t].reshape(L, L), mix[t]).astype(BF16)

    def held_part(t):
        held[t] = nn(cot[t, 0], qbuf[...].reshape(L, L)).astype(BF16)

    def gcross_part(t):
        gcv[t, 0] = tn(pbuf[:, t].reshape(L, L), held[t]).astype(BF16)

    for dy in order:
        d_in[dy].wait_recv()
    d_first(1)
    d_first(0)
    d_third(1)
    e_first()
    held_part(0)
    held_part(1)
    d_second(1)
    e_second()
    e_third()
    d_second(0)
    d_third(0)
    out_part(0)
    out_part(1)
    gcross_part(0)
    gcross_part(1)

    def d_final(chunk):
        total = d_local(0, chunk)
        for step in (1, -1, 2, -2):
            d_out[chunk, step].wait_recv()
            total += drecv[place(chunk, step)].astype(F32)
        return total

    dlast[0] = d_final(1).astype(BF16)
    dx = send(dlast.at[0], dlast.at[1], dx_s, dx_r, at_y(0, xh=1 - x_hi))
    total = e_local(0)
    for step in (1, -1, 2, -2):
        e_out[step].wait_recv()
        total += erecv[place(0, step)].astype(F32)
    gsup_ref[0] = soft_back(qbuf[t_id], total)
    d_own = d_final(0)
    dx.wait_recv()
    gtgt_ref[...] = soft_back(pbuf[s_id], d_own + dlast[1].astype(F32))

    for copy in pending:
        copy.wait_send()


def write_out(*refs):
    copies = [pltpu.make_async_copy(refs[i], refs[4 + i], refs[8].at[i]) for i in range(4)]
    for copy in copies:
        copy.start()
    for copy in copies:
        copy.wait()


def body(cross_kernel, cotangent, self_tgt, self_sup):
    vmem, dma = pltpu.VMEM, pltpu.SemaphoreType.DMA
    hbm_spec = pl.BlockSpec(memory_space=pltpu.HBM)
    vmem_spec = pl.BlockSpec(memory_space=pltpu.VMEM)
    docs = (2, 1, L, L)
    outs = (
        jax.ShapeDtypeStruct(docs, BF16),
        jax.ShapeDtypeStruct(docs, BF16),
        jax.ShapeDtypeStruct((2, 16, L), F32),
        jax.ShapeDtypeStruct((1, 32, L), F32),
    )
    results = pl.pallas_call(
        kernel,
        out_shape=outs,
        in_specs=[hbm_spec] * 4,
        out_specs=(vmem_spec,) * 4,
        scratch_shapes=[
            vmem(docs, BF16), vmem(docs, BF16), vmem((2, 16, L), BF16), vmem((1, 32, L), BF16),
            vmem((32, 2, 16, L), BF16), vmem((16, 32, L), BF16),
            vmem((2, L, L), BF16), vmem((2, L, L), BF16), vmem((2, L, L), BF16),
            vmem((2, 8, 2, 2, 16, L), BF16), vmem((8, 2, 2, 16, L), BF16),
            vmem((16, 32, L), BF16), vmem((8, 32, L), BF16),
            vmem((18, 2, 16, L), BF16), vmem((18, 2, 16, L), BF16),
            vmem((9, 32, L), BF16), vmem((9, 32, L), BF16),
            vmem((2, 2, 16, L), BF16),
            dma((4,)),
            dma, dma, dma((8,)), dma((8,)), dma((18,)), dma((18,)), dma((9,)), dma((9,)), dma((16,)), dma((16,)),
            dma((8,)), dma((8,)), dma((18,)), dma((18,)), dma((9,)), dma((9,)), dma, dma, dma((8,)), dma((8,)),
        ],
        compiler_params=pltpu.CompilerParams(
            collective_id=0, has_side_effects=True, vmem_limit_bytes=48 * 1024 * 1024
        ),
        name="layer",
    )(*[pltpu.with_memory_space_constraint(x, pltpu.HBM) for x in (cross_kernel, cotangent, self_tgt, self_sup)])
    return pl.pallas_call(
        write_out,
        out_shape=outs,
        in_specs=[vmem_spec] * 4,
        out_specs=(hbm_spec,) * 4,
        scratch_shapes=[dma((4,))],
        compiler_params=pltpu.CompilerParams(vmem_limit_bytes=1024 * 1024),
        name="write_out",
    )(*results)


def solution(mesh):
    in_specs = (
        P("tgt", "sup", None, None),
        P("tgt", "sup", None, None),
        P("tgt", "sup", None),
        P("sup", "tgt", None),
    )
    out_specs = (
        P("tgt", "sup", None, None),
        P("tgt", "sup", None, None),
        P("tgt", "sup", None),
        P("sup", "tgt", None),
    )
    return jax.shard_map(body, mesh=mesh, in_specs=in_specs, out_specs=out_specs, check_vma=False)
```

time: 53.2 us -> 46.7 us (0.88)
  Pallas kernels: 52.4 us -> 45.9 us
    pallas_call x1, Pallas kernels: 51 us -> 44.5 us  [body(): pl.pallas_call(kernel, out_shape=outs, in_specs=[hbm_spec] * 4, out_specs...]
where the time goes in v3:
time: 46.7 us; the launch traced here: 46.5 us
  Pallas kernels  45.9 us (98%)
  between operations  0.64 us (1%)
    pallas_call x1, Pallas kernels, body(): pl.pallas_call(kernel, out_shape=outs, in_specs=[hbm_spec] * 4, out_specs...  44.5 us
    pallas_call x1, Pallas kernels, body(): pl.pallas_call(write_out, out_shape=outs, in_specs=[vmem_spec] * 4, out_s...  1.38 us

profile of v3, /device:TPU:8, one launch (start us, length us, event | category | flops | bytes accessed | tf_op | source)
XLA Modules:
  0.0 46.5 jit_solution(8024608643708378234)
XLA Ops:
  0.6 44.5 %layer.1 = (bf16[2,1,512,512]{3,2,1,0:T(8,128)(2,1)S(1)}, bf16[2,1,512,512]{3,2,1,0:T(8,128)(2,1)S(1)}, f32[2,16,512]{2,1,0:T(8,128)S(1)}, f32[1,32,512]{2,1,0:T(8,128)S(1)}) custom-call(bf16[2,1,512,512]{3,2,1,0:T(8,128)(2,1)} %cross_hbm.1, bf16[2,1,512,512]{3,2,1,0:T(8,128)(2,1)} %cot_hbm.1, bf16[2,16,512]{2,1,0:T(8,128)(2,1)} %tgt_hbm.1, ...), custom_call_target="tpu_custom_call" | custom-call | tf_op jit(solution)/shard_map/layer/pallas_call | solution.py:387
  45.1 1.4 %write_out.1 = (bf16[2,1,512,512]{3,2,1,0:T(8,128)(2,1)}, bf16[2,1,512,512]{3,2,1,0:T(8,128)(2,1)}, f32[2,16,512]{2,1,0:T(8,128)}, f32[1,32,512]{2,1,0:T(8,128)}) custom-call(bf16[2,1,512,512]{3,2,1,0:T(8,128)(2,1)S(1)} %get-tuple-element.8.refs_0_, bf16[2,1,512,512]{3,2,1,0:T(8,128)(2,1)S(1)} %get-tuple-element.9.refs_1_, ...), custom_call_target="tpu_custom_call" | custom-call | tf_op jit(solution)/shard_map/write_out/pallas_call | solution.py:410

commit v4 on v3

--- a/solution.py
+++ b/solution.py
@@ -39,7 +39,7 @@
     cross_hbm, cot_hbm, tgt_hbm, sup_hbm,
     outv, gcv, gtgt_ref, gsup_ref,
     cross, cot, tgt_ref, sup_ref, pbuf, qbuf, mix, held, left,
-    dpart, dcore, epart, ecross, dstage, drecv, estage, erecv, dlast,
+    dpart, dcore, epart, ecross, dstage, drecv, estage, erecv, dlast, dxs, dcross,
     load_sem,
     px_s, px_r, qx_s, qx_r, pr_s, pr_r, qr_s, qr_r, pc_s, pc_r,
     dc_s, dc_r, dr_s, dr_r, er_s, er_r, dx_s, dx_r, ex_s, ex_r,
@@ -137,11 +137,18 @@
         i = len(c_copies)
         c_copies.append(send(pbuf.at[slot], pbuf.at[slot], pc_s.at[i], pc_r.at[i], at_y(0, c=1 - core)))
 
+    far = (4, 3, -3)
+    p_x = {}
+
+    def p_cross(dy):
+        slot, i = p_slot(dy, 0), (far + (0,)).index(dy)
+        p_x[dy] = send(pbuf.at[slot], pbuf.at[slot], px_s.at[i], px_r.at[i], at_y(0, xh=1 - x_hi))
+
     q_in, x_in, p_in = {}, [], {}
     for step in (2, -2, 1, -1):
         q_in[step] = q_send(0, step)
     x_in.append(q_cross(0))
-    px = send(pbuf.at[s_id], pbuf.at[s_id], px_s, px_r, at_y(0, xh=1 - x_hi))
+    p_cross(0)
     for step in (2, -2, 1, -1):
         p_in[0, step] = p_send(0, 0, step)
     p_core(0, 0)
@@ -164,20 +171,28 @@
     def p_second(chunk):
         for sign in (1, -1):
             p_in[chunk, 2 * sign].wait_recv()
-            p_in[chunk, 3 * sign] = p_send(chunk, -2 * sign, sign)
-            p_in[chunk, 4 * sign] = p_half(chunk, sign)
+            if chunk == 0:
+                p_in[0, 3 * sign] = p_send(0, -2 * sign, sign)
+                p_in[0, 4 * sign] = p_half(0, sign)
             p_core(-2 * sign, chunk)
 
-    def p_third(chunk):
-        for sign in (1, -1):
-            p_in[chunk, 3 * sign].wait_recv()
-            p_core(-3 * sign, chunk)
-        for sign in (1, -1):
-            p_in[chunk, 4 * sign].wait_recv()
-        p_core(4, chunk)
+    def p_third():
+        for sign in (1, -1):
+            p_in[0, 3 * sign].wait_recv()
+            p_cross(-3 * sign)
+            p_core(-3 * sign, 0)
+        for sign in (1, -1):
+            p_in[0, 4 * sign].wait_recv()
+        p_cross(4)
+        p_core(4, 0)
+
+    def p_last():
+        for dy in (-3, 3, 4):
+            p_x[dy].wait_recv()
+            p_core(dy, 1)
 
     p_second(0)
-    px.wait_recv()
+    p_x[0].wait_recv()
     for step in (2, -2, 1, -1):
         p_in[1, step] = p_send(1, 0, step)
     p_core(0, 1)
@@ -187,7 +202,7 @@
     for sign in (1, -1):
         q_in[4 * sign].wait_recv()
     x_in.append(q_cross(4))
-    p_third(0)
+    p_third()
     for sign in (1, -1):
         p_in[1, sign].wait_recv()
         p_core(-sign, 1)
@@ -198,7 +213,6 @@
     q_all = qbuf[...].reshape(L, L)
     for t in range(2):
         mix[t] = nt(cross[t, 0], q_all).astype(BF16)
-    p_third(1)
     for t in range(2):
         d = nt(cot[t, 0], mix[t]).astype(BF16)
         for s in range(32):
@@ -212,18 +226,7 @@
             dpart.at[1 - core, dest], dcore.at[dest], dc_s.at[i], dc_r.at[i], at_y(0, c=1 - core)
         )
 
-    for c in c_copies:
-        c.wait_recv()
-    for t in range(2):
-        p_t = pbuf[:, t].reshape(L, L)
-        left[t] = nn(p_t, cross[t, 0]).astype(BF16)
-    e = tn(cot[0, 0], left[0]) + tn(cot[1, 0], left[1])
-    epart[...] = e.astype(BF16).reshape(16, 32, L)
-
     e_in = {}
-    for i, dz in enumerate(order):
-        slot = q_slot(dz, 1)
-        e_in[dz] = send(epart.at[slot], ecross.at[i], ex_s.at[i], ex_r.at[i], at_z(0, xl=1 - x_lo))
 
     def d_local(dy, chunk):
         dest = (y + dy + RING) % RING
@@ -260,12 +263,25 @@
             estage.at[i, rows], erecv.at[i, rows], er_s.at[j], er_r.at[j], at_z(2 * sign)
         )
 
+    d_x = {}
+
+    def d_cross():
+        for i, dy in enumerate(far):
+            dxs[i] = d_local(dy, 1).astype(BF16)
+            d_x[dy] = send(dxs.at[i], dcross.at[i], dx_s.at[i], dx_r.at[i], at_y(0, xh=1 - x_hi))
+        for step in (2, -2, 1, -1):
+            d_send(1, step, step, d_local(step, 1))
+
+    def d_far(dy):
+        d_x[dy].wait_recv()
+        return d_local(dy, 0) + dcross[far.index(dy)].astype(F32)
+
     def d_first(chunk):
-        dstage[place(chunk, 4)] = d_local(4, chunk).astype(BF16)
+        dstage[place(chunk, 4)] = d_far(4).astype(BF16)
         for sign in (1, -1):
             d_half(chunk, sign)
         for sign in (1, -1):
-            d_send(chunk, 3 * sign, sign, d_local(3 * sign, chunk))
+            d_send(chunk, 3 * sign, sign, d_far(3 * sign))
 
     def d_second(chunk):
         for sign in (1, -1):
@@ -316,6 +332,22 @@
         for sign in (1, -1):
             e_send(sign, sign, e_local(sign))
 
+    for dy in order:
+        d_in[dy].wait_recv()
+    d_cross()
+    p_last()
+    for c in c_copies:
+        c.wait_recv()
+    for t in range(2):
+        p_t = pbuf[:, t].reshape(L, L)
+        left[t] = nn(p_t, cross[t, 0]).astype(BF16)
+    e = tn(cot[0, 0], left[0]) + tn(cot[1, 0], left[1])
+    epart[...] = e.astype(BF16).reshape(16, 32, L)
+
+    for i, dz in enumerate(order):
+        slot = q_slot(dz, 1)
+        e_in[dz] = send(epart.at[slot], ecross.at[i], ex_s.at[i], ex_r.at[i], at_z(0, xl=1 - x_lo))
+
     def out_part(t):
         outv[t, 0] = nn(pbuf[:, t].reshape(L, L), mix[t]).astype(BF16)
 
@@ -324,24 +356,6 @@
 
     def gcross_part(t):
         gcv[t, 0] = tn(pbuf[:, t].reshape(L, L), held[t]).astype(BF16)
-
-    for dy in order:
-        d_in[dy].wait_recv()
-    d_first(1)
-    d_first(0)
-    d_third(1)
-    e_first()
-    held_part(0)
-    held_part(1)
-    d_second(1)
-    e_second()
-    e_third()
-    d_second(0)
-    d_third(0)
-    out_part(0)
-    out_part(1)
-    gcross_part(0)
-    gcross_part(1)
 
     def d_final(chunk):
         total = d_local(0, chunk)
@@ -350,16 +364,28 @@
             total += drecv[place(chunk, step)].astype(F32)
         return total
 
+    d_first(0)
+    held_part(0)
+    e_first()
+    held_part(1)
+    d_third(0)
     dlast[0] = d_final(1).astype(BF16)
-    dx = send(dlast.at[0], dlast.at[1], dx_s, dx_r, at_y(0, xh=1 - x_hi))
+    dx = send(dlast.at[0], dlast.at[1], dx_s.at[3], dx_r.at[3], at_y(0, xh=1 - x_hi))
+    out_part(0)
+    d_second(0)
+    e_second()
+    e_third()
+    out_part(1)
+    gcross_part(0)
+    gcross_part(1)
+    d_own = d_final(0)
+    dx.wait_recv()
+    gtgt_ref[...] = soft_back(pbuf[s_id], d_own + dlast[1].astype(F32))
     total = e_local(0)
     for step in (1, -1, 2, -2):
         e_out[step].wait_recv()
         total += erecv[place(0, step)].astype(F32)
     gsup_ref[0] = soft_back(qbuf[t_id], total)
-    d_own = d_final(0)
-    dx.wait_recv()
-    gtgt_ref[...] = soft_back(pbuf[s_id], d_own + dlast[1].astype(F32))
 
     for copy in pending:
         copy.wait_send()
@@ -397,10 +423,10 @@
             vmem((16, 32, L), BF16), vmem((8, 32, L), BF16),
             vmem((18, 2, 16, L), BF16), vmem((18, 2, 16, L), BF16),
             vmem((9, 32, L), BF16), vmem((9, 32, L), BF16),
-            vmem((2, 2, 16, L), BF16),
+            vmem((2, 2, 16, L), BF16), vmem((3, 2, 16, L), BF16), vmem((3, 2, 16, L), BF16),
             dma((4,)),
-            dma, dma, dma((8,)), dma((8,)), dma((18,)), dma((18,)), dma((9,)), dma((9,)), dma((16,)), dma((16,)),
-            dma((8,)), dma((8,)), dma((18,)), dma((18,)), dma((9,)), dma((9,)), dma, dma, dma((8,)), dma((8,)),
+            dma((4,)), dma((4,)), dma((8,)), dma((8,)), dma((18,)), dma((18,)), dma((9,)), dma((9,)), dma((16,)), dma((16,)),
+            dma((8,)), dma((8,)), dma((18,)), dma((18,)), dma((9,)), dma((9,)), dma((4,)), dma((4,)), dma((8,)), dma((8,)),
         ],
         compiler_params=pltpu.CompilerParams(
             collective_id=0, has_side_effects=True, vmem_limit_bytes=48 * 1024 * 1024

time: 46.7 us -> 46.1 us (0.987)
  the two profiles are of different devices: /device:TPU:8 before, /device:TPU:4 now
where the time goes in v4:
time: 46.1 us; the launch traced here: 45.9 us
  Pallas kernels  45.3 us (98%)
  between operations  0.64 us (1%)
    pallas_call x1, Pallas kernels, body(): pl.pallas_call(kernel, out_shape=outs, in_specs=[hbm_spec] * 4, out_specs...  43.9 us
    pallas_call x1, Pallas kernels, body(): pl.pallas_call(write_out, out_shape=outs, in_specs=[vmem_spec] * 4, out_s...  1.38 us

profile of v4, /device:TPU:4, one launch (start us, length us, event | category | flops | bytes accessed | tf_op | source)
XLA Modules:
  0.0 45.9 jit_solution(609401655004281089)
XLA Ops:
  0.6 43.9 %layer.1 = (bf16[2,1,512,512]{3,2,1,0:T(8,128)(2,1)S(1)}, bf16[2,1,512,512]{3,2,1,0:T(8,128)(2,1)S(1)}, f32[2,16,512]{2,1,0:T(8,128)S(1)}, f32[1,32,512]{2,1,0:T(8,128)S(1)}) custom-call(bf16[2,1,512,512]{3,2,1,0:T(8,128)(2,1)} %cross_hbm.1, bf16[2,1,512,512]{3,2,1,0:T(8,128)(2,1)} %cot_hbm.1, bf16[2,16,512]{2,1,0:T(8,128)(2,1)} %tgt_hbm.1, ...), custom_call_target="tpu_custom_call" | custom-call | tf_op jit(solution)/shard_map/layer/pallas_call | solution.py:413
  44.6 1.4 %write_out.1 = (bf16[2,1,512,512]{3,2,1,0:T(8,128)(2,1)}, bf16[2,1,512,512]{3,2,1,0:T(8,128)(2,1)}, f32[2,16,512]{2,1,0:T(8,128)}, f32[1,32,512]{2,1,0:T(8,128)}) custom-call(bf16[2,1,512,512]{3,2,1,0:T(8,128)(2,1)S(1)} %get-tuple-element.8.refs_0_, bf16[2,1,512,512]{3,2,1,0:T(8,128)(2,1)S(1)} %get-tuple-element.9.refs_1_, ...), custom_call_target="tpu_custom_call" | custom-call | tf_op jit(solution)/shard_map/write_out/pallas_call | solution.py:436

commit v5 on v4

--- a/solution.py
+++ b/solution.py
@@ -211,8 +211,7 @@
     for c in x_in:
         c.wait_recv()
     q_all = qbuf[...].reshape(L, L)
-    for t in range(2):
-        mix[t] = nt(cross[t, 0], q_all).astype(BF16)
+    mix[...] = nt(cross[...].reshape(2 * L, L), q_all).astype(BF16).reshape(2, L, L)
     for t in range(2):
         d = nt(cot[t, 0], mix[t]).astype(BF16)
         for s in range(32):
@@ -341,7 +340,7 @@
     for t in range(2):
         p_t = pbuf[:, t].reshape(L, L)
         left[t] = nn(p_t, cross[t, 0]).astype(BF16)
-    e = tn(cot[0, 0], left[0]) + tn(cot[1, 0], left[1])
+    e = tn(cot[...].reshape(2 * L, L), left[...].reshape(2 * L, L))
     epart[...] = e.astype(BF16).reshape(16, 32, L)
 
     for i, dz in enumerate(order):

time: 46.1 us -> 46 us (level)
  no operation moved by 1% of the time
where the time goes in v5:
time: 46 us; the launch traced here: 45.9 us
  Pallas kernels  45.2 us (98%)
  between operations  0.64 us (1%)
    pallas_call x1, Pallas kernels, body(): pl.pallas_call(kernel, out_shape=outs, in_specs=[hbm_spec] * 4, out_specs...  43.8 us
    pallas_call x1, Pallas kernels, body(): pl.pallas_call(write_out, out_shape=outs, in_specs=[vmem_spec] * 4, out_s...  1.38 us

profile of v5, /device:TPU:4, one launch (start us, length us, event | category | flops | bytes accessed | tf_op | source)
XLA Modules:
  0.0 45.9 jit_solution(6150601976185990644)
XLA Ops:
  0.6 43.8 %layer.1 = (bf16[2,1,512,512]{3,2,1,0:T(8,128)(2,1)S(1)}, bf16[2,1,512,512]{3,2,1,0:T(8,128)(2,1)S(1)}, f32[2,16,512]{2,1,0:T(8,128)S(1)}, f32[1,32,512]{2,1,0:T(8,128)S(1)}) custom-call(bf16[2,1,512,512]{3,2,1,0:T(8,128)(2,1)} %cross_hbm.1, bf16[2,1,512,512]{3,2,1,0:T(8,128)(2,1)} %cot_hbm.1, bf16[2,16,512]{2,1,0:T(8,128)(2,1)} %tgt_hbm.1, ...), custom_call_target="tpu_custom_call" | custom-call | tf_op jit(solution)/shard_map/layer/pallas_call | solution.py:412
  44.5 1.4 %write_out.1 = (bf16[2,1,512,512]{3,2,1,0:T(8,128)(2,1)}, bf16[2,1,512,512]{3,2,1,0:T(8,128)(2,1)}, f32[2,16,512]{2,1,0:T(8,128)}, f32[1,32,512]{2,1,0:T(8,128)}) custom-call(bf16[2,1,512,512]{3,2,1,0:T(8,128)(2,1)S(1)} %get-tuple-element.8.refs_0_, bf16[2,1,512,512]{3,2,1,0:T(8,128)(2,1)S(1)} %get-tuple-element.9.refs_1_, ...), custom_call_target="tpu_custom_call" | custom-call | tf_op jit(solution)/shard_map/write_out/pallas_call | solution.py:435
